TPU v7x, 256 devices: a whole 4x4x8 slice. The times are simulated.
256 devices in a mesh: seq: 64 (over x, y, z_hi, core), head: 4 (over z_lo).
Axes of the slice: x: 4, y: 4, z: 8 (z_hi: 2, z_lo: 4; z = z_hi * 4 + z_lo), core: 2. Of those that a mesh axis runs over, the one named last changes fastest.
Arguments:
- q_rows: float32 [16384, 2048], P(('seq', 'head')), may hold values from -4 to 4
- k_rows: float32 [16384, 2048], P(('seq', 'head')), may hold values from -4 to 4
- v_rows: float32 [16384, 2048], P(('seq', 'head')), may hold values from -6 to 6
- step_sizes: float32 [8, 16384], P('head', 'seq'), may hold values from 0.1 to 1
- fast_weights: float32 [3, 8, 256, 512], P(None, 'head'), may hold values from -0.375 to 0.375
- norm_gain: float32 [2048], P('head'), may hold values from 0.1 to 1.9
- w_out: bfloat16 [2048, 4096], P('head'), may hold values from -0.125 to 0.125
Outputs:
- mixed_out: bfloat16 [16384, 4096], P(('seq', 'head'))
- new_weights: float32 [3, 8, 256, 512], P(None, 'head')
All inputs are finite; a program needn't handle non-finite values.
Results may differ from a plain program's by a relative error of at most 0.005.
Values sent between devices are 32-bit elements; how exact they have to be, the bound alone decides.
No kernel may reach another device: no remote copies, remote signals or barrier semaphores. Data moves between devices by JAX's collectives and lax.ppermute only.
A program may use at most 128 MiB of HBM per device.

v0:
```python
import math
import jax
import jax.numpy as jnp
from jax import lax
from jax.experimental import pallas as pl
from jax.experimental.pallas import tpu as pltpu
from jax.sharding import Mesh, PartitionSpec as P


NS_ITERS = 3
epsilon = 1e-06
coef_linear = 3.4445
coef_square = -4.775
coef_cubic = 2.0315


def split(value):
    high = value.astype(jnp.bfloat16)
    low = (value - high.astype(jnp.float32)).astype(jnp.bfloat16)
    return high, low


def dot3(left, right, contract):
    dims = (contract, ((), ()))
    (lh, ll), (rh, rl) = left, right
    prod = lambda a, b: lax.dot_general(a, b, dims, preferred_element_type=jnp.float32)
    return prod(lh, rh) + (prod(lh, rl) + prod(ll, rh))


NN = ((1,), (0,))
NT = ((1,), (1,))
TN = ((0,), (0,))


def rows_of(ref):
    return ref[...].reshape(-1, ref.shape[-1])


def joined(*refs):
    return jnp.concatenate([ref[...] for ref in refs], axis=0)


def gradient_kernel(k_ref, v_ref, s_ref, w_ref, g_ref):
    key = split(rows_of(k_ref))
    upstream = split(-s_ref[...] * rows_of(v_ref))
    gate_pre = dot3(key, split(w_ref[0]), NN)
    up_pre = dot3(key, split(w_ref[2]), NN)
    back = dot3(upstream, split(w_ref[1]), NN)
    sig = jax.nn.sigmoid(gate_pre)
    active = gate_pre * sig
    g_ref[1] = dot3(upstream, split(active * up_pre), TN)
    g_ref[2] = dot3(key, split(back * active), TN)
    slope = sig * (1.0 + gate_pre * (1.0 - sig))
    g_ref[0] = dot3(key, split(back * up_pre * slope), TN)


def newton_kernel(g_ref, w_ref, o_ref):
    mats = []
    for i in range(3):
        g = g_ref[i]
        mats.append(g * (1.0 / (jnp.sqrt(jnp.sum(g * g, keepdims=True)) + epsilon)))
    for _ in range(NS_ITERS):
        parts = [split(m) for m in mats]
        grams = [dot3(p, p, NT) for p in parts]
        gparts = [split(a) for a in grams]
        polys = [coef_square * a + coef_cubic * dot3(p, p, NN) for a, p in zip(grams, gparts)]
        mats = [coef_linear * m + dot3(split(b), p, NN) for m, b, p in zip(mats, polys, parts)]
    for i in range(3):
        w = w_ref[i]
        c = w - mats[i]
        target = jnp.sqrt(jnp.sum(w * w, axis=0, keepdims=True))
        current = jnp.sqrt(jnp.sum(c * c, axis=0, keepdims=True)) + epsilon
        o_ref[i] = c * (target / current)


def attention_kernel(first_ref, order_ref, qa, qb, qc, qd, kp_ref, k_ref, vp_ref, v_ref, o_ref):
    q = split(joined(qa, qb, qc, qd))
    scale = 1.0 / math.sqrt(o_ref.shape[-1])
    prev = dot3(q, split(rows_of(kp_ref)), NT) * scale
    here = dot3(q, split(rows_of(k_ref)), NT) * scale
    row = lax.broadcasted_iota(jnp.int32, prev.shape, 0)
    col = lax.broadcasted_iota(jnp.int32, prev.shape, 1)
    prev = jnp.where((col > row) & (first_ref[0] > 0), prev, -1e30)
    here = jnp.where(col <= row, here, -1e30)
    top = jnp.maximum(jnp.max(prev, axis=1, keepdims=True), jnp.max(here, axis=1, keepdims=True))
    ep, eh = jnp.exp(prev - top), jnp.exp(here - top)
    total = jnp.sum(ep, axis=1, keepdims=True) + jnp.sum(eh, axis=1, keepdims=True)
    acc = dot3(split(ep), split(rows_of(vp_ref)), NN) + dot3(split(eh), split(rows_of(v_ref)), NN)
    o_ref[...] = acc / total


def apply_head(qa, qb, qc, qd, w_ref, att_ref, gain_ref):
    q = split(joined(qa, qb, qc, qd))
    gate_pre = dot3(q, split(w_ref[0]), NN)
    up_pre = dot3(q, split(w_ref[2]), NN)
    glu = gate_pre * jax.nn.sigmoid(gate_pre) * up_pre
    fast = dot3(split(glu), split(w_ref[1]), NT)
    fast = fast * lax.rsqrt(jnp.mean(fast * fast, axis=1, keepdims=True) + epsilon)
    return fast * gain_ref[...] + att_ref[...]


def apply_first_kernel(head_ref, order_ref, *refs):
    *given, o_ref = refs
    o_ref[...] = apply_head(*given)


def apply_second_kernel(head_ref, order_ref, *refs):
    *given, done_ref, o_ref = refs
    value = apply_head(*given)
    done = done_ref[...]
    is_first = head_ref[0] == 0
    dim = value.shape[1]
    shape = (o_ref.shape[0], o_ref.shape[1], dim)
    o_ref[:, :, :dim] = jnp.where(is_first, value, done).reshape(shape)
    o_ref[:, :, dim:] = jnp.where(is_first, done, value).reshape(shape)


def slice_kernel(place_ref, w_ref, o_ref):
    o_ref[...] = w_ref[...].astype(jnp.float32)


def project_kernel(place_ref, order_ref, *refs):
    lefts, (far_ref, near_ref, mine_ref, theirs_ref) = refs[:8], refs[8:]
    total = None
    for slot in range(4):
        rows = jnp.concatenate([lefts[slot][...], lefts[4 + slot][...]], axis=0)
        right = near_ref[...] if slot == 0 else rows_of(far_ref.at[:, slot - 1]).astype(jnp.bfloat16)
        value = jnp.dot(rows.astype(jnp.bfloat16), right, preferred_element_type=jnp.float32)
        total = value if total is None else total + value
    half = total.shape[0] // 2
    mine_ref[...] = total[:half]
    theirs_ref[...] = total[half:]


def finish_kernel(place_ref, mine_ref, given_ref, o_ref):
    is_first = place_ref[0] == 0
    mine, given = mine_ref[...], given_ref[...]
    width = mine.shape[1]
    o_ref[:, :width] = jnp.where(is_first, mine, given).astype(o_ref.dtype)
    o_ref[:, width:] = jnp.where(is_first, given, mine).astype(o_ref.dtype)


def assemble_kernel(place_ref, mine_ref, given_ref, o_ref):
    is_first = place_ref[0] == 0
    mine, given = mine_ref[...], given_ref[...]
    o_ref[:, 0] = jnp.where(is_first, mine, given)
    o_ref[:, 1] = jnp.where(is_first, given, mine)


SEQ = ("x", "y", "zh", "core")
HEAD_DIM = 256
PARAMS = pltpu.CompilerParams(vmem_limit_bytes=24 * 2**20)


def head_gradient(pairs, steps, weights, head):
    dim, hidden = weights.shape[2:]
    length = steps.shape[1]
    ranks, _, rows, _ = pairs.shape
    spec = pltpu.PrefetchScalarGridSpec(
        num_scalar_prefetch=1,
        grid=(1,),
        in_specs=[
            pl.BlockSpec((ranks, None, rows, dim), lambda i, h: (0, 0, 0, h[0])),
            pl.BlockSpec((ranks, None, rows, dim), lambda i, h: (0, 1, 0, h[0])),
            pl.BlockSpec((None, length, 1), lambda i, h: (h[0], 0, 0)),
            pl.BlockSpec((3, None, dim, hidden), lambda i, h: (0, h[0], 0, 0)),
        ],
        out_specs=pl.BlockSpec((3, dim, hidden), lambda i, h: (0, 0, 0)),
    )
    return pl.pallas_call(
        lambda h, *refs: gradient_kernel(*refs),
        grid_spec=spec,
        out_shape=jax.ShapeDtypeStruct((3, dim, hidden), jnp.float32),
        compiler_params=PARAMS,
        name="gradient",
    )(head, pairs, pairs, steps, in_hbm(weights))


def newton(grads, weights, head):
    _, dim, hidden = grads.shape
    spec = pltpu.PrefetchScalarGridSpec(
        num_scalar_prefetch=1,
        grid=(1,),
        in_specs=[
            pl.BlockSpec((3, dim, hidden), lambda i, h: (0, 0, 0)),
            pl.BlockSpec((3, None, dim, hidden), lambda i, h: (0, h[0], 0, 0)),
        ],
        out_specs=pl.BlockSpec((3, dim, hidden), lambda i, h: (0, 0, 0)),
    )
    return pl.pallas_call(
        lambda h, *refs: newton_kernel(*refs),
        grid_spec=spec,
        out_shape=jax.ShapeDtypeStruct((3, dim, hidden), jnp.float32),
        compiler_params=PARAMS,
        name="newton",
    )(head, in_hbm(grads), in_hbm(weights))


def query_specs(rows, dim, column):
    def block(source):
        return pl.BlockSpec(
            (None, rows, dim), lambda i, f, order: (order[source], 0, column(i, f))
        )

    return [block(source) for source in range(4)]


def attention(first, order, queries, before, pairs):
    ranks, _, rows, width = pairs.shape
    dim = HEAD_DIM
    length = ranks * rows
    key = pl.BlockSpec((ranks, None, rows, dim), lambda i, f, order: (0, 0, 0, i))
    value = pl.BlockSpec((ranks, None, rows, dim), lambda i, f, order: (0, 1, 0, i))
    return pl.pallas_call(
        attention_kernel,
        grid_spec=pltpu.PrefetchScalarGridSpec(
            num_scalar_prefetch=2,
            grid=(width // dim,),
            in_specs=[*query_specs(rows, dim, lambda i, f: i), key, key, value, value],
            out_specs=pl.BlockSpec((length, dim), lambda i, f, order: (0, i)),
        ),
        out_shape=jax.ShapeDtypeStruct((length, width), jnp.float32),
        compiler_params=PARAMS,
        name="attention",
    )(first, order, *[queries] * 4, before, pairs, before, pairs)


def apply_fast(head, order, queries, weights, attended, gain, done=None):
    ranks, rows, width = queries.shape
    length = ranks * rows
    _, dim, hidden = weights.shape
    specs = [
        *query_specs(rows, dim, lambda i, h: h[0]),
        pl.BlockSpec((3, dim, hidden), lambda i, h, order: (0, 0, 0)),
        pl.BlockSpec((length, dim), lambda i, h, order: (0, h[0])),
        pl.BlockSpec((1, dim), lambda i, h, order: (0, h[0])),
    ]
    if done is not None:
        specs.append(pl.BlockSpec((length, dim), lambda i, h, order: (0, 0)))
    if done is None:
        out_shape = (length, dim)
    else:
        out_shape = (ranks, rows, width)
    return pl.pallas_call(
        apply_first_kernel if done is None else apply_second_kernel,
        grid_spec=pltpu.PrefetchScalarGridSpec(
            num_scalar_prefetch=2,
            grid=(1,),
            in_specs=specs,
            out_specs=pl.BlockSpec(out_shape, lambda i, h, order: (0,) * len(out_shape)),
        ),
        out_shape=jax.ShapeDtypeStruct(out_shape, jnp.float32),
        compiler_params=PARAMS,
    )(head, order, *[queries] * 4, weights, attended, gain, *(() if done is None else (done,)))


def weight_slice(w_out, part, core):
    rows, width = w_out.shape[0] // 16, w_out.shape[1] // 2
    place = jnp.stack([part, core])
    return pl.pallas_call(
        slice_kernel,
        grid_spec=pltpu.PrefetchScalarGridSpec(
            num_scalar_prefetch=1,
            grid=(1,),
            in_specs=[pl.BlockSpec((rows, width), lambda i, p: (p[0], p[1]))],
            out_specs=pl.BlockSpec((rows, width), lambda i, p: (0, 0)),
        ),
        out_shape=jax.ShapeDtypeStruct((rows, width), jnp.float32),
        compiler_params=PARAMS,
        name="weight_slice",
    )(place, in_hbm(w_out))


def project(core, order, mine, theirs, far, near):
    _, rows, dim = mine.shape
    parts, others, piece, width = far.shape
    block = width // 4

    def left(slot):
        return pl.BlockSpec((None, rows, dim), lambda i, c, order: (order[slot], 0, 0))

    out = pl.BlockSpec((rows, block), lambda i, c, order: (0, i))
    return pl.pallas_call(
        project_kernel,
        grid_spec=pltpu.PrefetchScalarGridSpec(
            num_scalar_prefetch=2,
            grid=(width // block,),
            in_specs=[
                *[left(slot) for slot in range(4)] * 2,
                pl.BlockSpec((parts, others, piece, block), lambda i, c, order: (0, 0, 0, i)),
                pl.BlockSpec((dim, block), lambda i, c, order: (0, c[0] * (width // block) + i)),
            ],
            out_specs=[out, out],
        ),
        out_shape=[jax.ShapeDtypeStruct((rows, width), jnp.float32)] * 2,
        compiler_params=pltpu.CompilerParams(vmem_limit_bytes=40 * 2**20),
        name="project",
    )(core, order, *[mine] * 4, *[theirs] * 4, in_hbm(far), in_hbm(near))


def finish(core, mine, given):
    rows, width = mine.shape
    block = pl.BlockSpec((rows, width), lambda i, c: (0, 0))
    return pl.pallas_call(
        finish_kernel,
        grid_spec=pltpu.PrefetchScalarGridSpec(
            num_scalar_prefetch=1,
            grid=(1,),
            in_specs=[block, block],
            out_specs=pl.BlockSpec((rows, 2 * width), lambda i, c: (0, 0)),
        ),
        out_shape=jax.ShapeDtypeStruct((rows, 2 * width), jnp.bfloat16),
        compiler_params=PARAMS,
        name="finish",
    )(core, mine, given)


def assemble(core, mine, given):
    kinds, dim, hidden = mine.shape
    block = pl.BlockSpec((1, dim, hidden), lambda i, c: (i, 0, 0))
    return pl.pallas_call(
        assemble_kernel,
        grid_spec=pltpu.PrefetchScalarGridSpec(
            num_scalar_prefetch=1,
            grid=(kinds,),
            in_specs=[block, block],
            out_specs=pl.BlockSpec((1, 2, dim, hidden), lambda i, c: (i, 0, 0, 0)),
        ),
        out_shape=jax.ShapeDtypeStruct((kinds, 2, dim, hidden), jnp.float32),
        compiler_params=PARAMS,
        name="assemble",
    )(core, mine, given)


def by_head(rows):
    length, width = rows.shape
    return rows.reshape(length, 4, width // 4).transpose(1, 0, 2)


def exchange(value, axes):
    return lax.all_to_all(value, axes, split_axis=0, concat_axis=0, tiled=True)


def turned(value, step):
    return lax.ppermute(value, "head", [(rank, (rank + step) % 4) for rank in range(4)])


def rotated_heads(rows):
    width = rows.shape[1] // 4
    here = lax.axis_index("head")
    parts = []
    for step in range(4):
        column = lax.rem(here + step, 4) * width
        part = lax.dynamic_slice_in_dim(rows, column, width, axis=1)
        parts.append(turned(part, step) if step else part)
    order = jnp.stack([lax.rem(here + 4 - source, 4) for source in range(4)])
    return jnp.stack(parts), order


def in_hbm(value):
    return pltpu.with_memory_space_constraint(value, pltpu.HBM)


def swap_cores(value):
    return lax.ppermute(value, "core", [(0, 1), (1, 0)])


def sum_rest(value):
    shape = value.shape
    pieces = exchange(value.reshape(16, -1, shape[-1]), ("x", "y"))
    part = jnp.sum(pieces, axis=0)
    part = part + lax.ppermute(part, "zh", [(0, 1), (1, 0)])
    return exchange(jnp.broadcast_to(part, (16, *part.shape)), ("x", "y")).reshape(shape)


def earlier(value):
    return lax.ppermute(value, SEQ, [(source, source + 1) for source in range(63)])


def local(q_rows, k_rows, v_rows, step_sizes, fast_weights, norm_gain, w_out):
    core, here = lax.axis_index("core"), lax.axis_index("head")
    mine, other = core.reshape(1), (1 - core).reshape(1)
    first = lax.axis_index(SEQ).reshape(1)
    steps = step_sizes[:, :, None]
    gain = norm_gain.reshape(1, -1)
    pairs = exchange(jnp.stack([by_head(k_rows), by_head(v_rows)], axis=1), "head")
    part = weight_slice(w_out, lax.axis_index("x") * 4 + lax.axis_index("y"), core)
    far_part = jnp.stack([turned(part, step) for step in (1, 2, 3)])
    far_weights = lax.all_gather(far_part, ("x", "y"))
    given = head_gradient(pairs, steps, fast_weights, other)
    received = swap_cores(given)
    kept = head_gradient(pairs, steps, fast_weights, mine)
    before = earlier(pairs)
    total = sum_rest(kept + received)
    updated = newton(total, fast_weights, mine)
    partner = swap_cores(updated)
    queries, order = rotated_heads(q_rows)
    attended = attention(first, order, queries, before, pairs)
    done = apply_fast(mine, order, queries, updated, attended, gain)
    combined = apply_fast(other, order, queries, partner, attended, gain, done)
    own_rows = exchange(combined, "head")
    their_rows = swap_cores(own_rows)
    turn = jnp.stack([lax.rem(here + 4 - step, 4) for step in range(4)])
    kept_out, given_out = project(mine, turn, own_rows, their_rows, far_weights, w_out)
    other_half = swap_cores(given_out)
    mixed = finish(mine, kept_out, other_half)
    new_weights = assemble(mine, in_hbm(updated), in_hbm(partner))
    return (mixed, new_weights)


def solution(mesh):
    mesh = Mesh(mesh.devices.reshape(4, 4, 2, 2, 4), (*SEQ, "head"))
    return jax.shard_map(
        local,
        mesh=mesh,
        in_specs=(
            P((*SEQ, "head"), None),
            P((*SEQ, "head"), None),
            P((*SEQ, "head"), None),
            P("head", SEQ),
            P(None, "head", None, None),
            P("head"),
            P("head", None),
        ),
        out_specs=(P((*SEQ, "head"), None), P(None, "head", None, None)),
        check_vma=False,
    )
```

profile of v0, /device:TPU:1, one launch (start us, length us, event | category | flops | bytes accessed | tf_op | source)
XLA Modules:
  0.0 267.2 jit_solution(14675265452661586217)
XLA Ops:
  8.8 2.5 collective-permute-start.8
  11.3 3.0 %collective-permute-start.9 = (f32[32,2048]{1,0:T(8,128)S(1)}, f32[32,2048]{1,0:T(8,128)S(1)}, u32[]{:S(2)}, u32[]{:S(2)}) collective-permute-start(f32[32,2048]{1,0:T(8,128)S(1)} %weight_slice.1), channel_id=1, source_target_pairs={{0,2},{1,3},{2,0},{3,1},{4,6},{5,7},{6,4},{7,5},{8,10},{9,11},{10,... | collective-permute-start | bytes 786440 | tf_op jit(solution)/shard_map/ppermute | solution.py:345
  15.0 4.1 %collective-permute-done.8 = f32[32,2048]{1,0:T(8,128)S(1)} collective-permute-done((f32[32,2048]{1,0:T(8,128)S(1)}, f32[32,2048]{1,0:T(8,128)S(1)}, u32[]{:S(2)}, u32[]{:S(2)}) %collective-permute-start.8) | collective-permute-done | bytes 262176 | tf_op jit(solution)/shard_map/ppermute | solution.py:345
  19.2 12.9 %collective-permute-done.9 = f32[32,2048]{1,0:T(8,128)S(1)} collective-permute-done((f32[32,2048]{1,0:T(8,128)S(1)}, f32[32,2048]{1,0:T(8,128)S(1)}, u32[]{:S(2)}, u32[]{:S(2)}) %collective-permute-start.9) | collective-permute-done | bytes 262176 | tf_op jit(solution)/shard_map/ppermute | solution.py:345
  34.2 7.3 %all-to-all-start = ((f32[4,2,64,512]{3,2,1,0:T(8,128)}), f32[4,2,64,512]{3,2,1,0:T(8,128)S(1)}, u32[]{:S(2)}, u32[]{:S(2)}) async-start(f32[4,2,64,512]{3,2,1,0:T(8,128)} %pad_maximum_fusion), calls=%async_computation | async-start | bytes 2097152 | tf_op jit(solution)/shard_map/all_to_all | solution.py:341
  41.7 25.2 %all-to-all-done.refs_0_.refs_1_.k_ref.v_ref = f32[4,2,64,512]{3,2,1,0:T(8,128)S(1)} async-done(((f32[4,2,64,512]{3,2,1,0:T(8,128)}), f32[4,2,64,512]{3,2,1,0:T(8,128)S(1)}, u32[]{:S(2)}, u32[]{:S(2)}) %all-to-all-start) | async-done | bytes 1048608 | tf_op jit(solution)/shard_map/all_to_all | solution.py:341
  66.9 3.0 %gradient.3 = f32[3,256,512]{2,1,0:T(8,128)S(1)} custom-call(s32[1]{0:T(128)} %bitcast.5.h.head_ref, f32[4,2,64,512]{3,2,1,0:T(8,128)S(1)} %all-to-all-done.refs_0_.refs_1_.k_ref.v_ref, f32[4,2,64,512]{3,2,1,0:T(8,128)S(1)} %all-to-all-done.refs_0_.refs_1_.k_ref.v_ref, f32[2,256,1]{2,1,0:T(8,128)S(1)} %copy.15.refs_2_, f32[3,2,256,512]{3,2,1,0:T(8,128)} %refs_1_.1), custom_call_target="tpu_custom_call" | custom-call | tf_op jit(solution)/shard_map/gradient/pallas_call | solution.py:170
  71.3 3.0 %gradient.2 = f32[3,256,512]{2,1,0:T(8,128)S(1)} custom-call(s32[1]{0:T(128)} %bitcast.h.head_ref.place_ref, f32[4,2,64,512]{3,2,1,0:T(8,128)S(1)} %all-to-all-done.refs_0_.refs_1_.k_ref.v_ref, f32[4,2,64,512]{3,2,1,0:T(8,128)S(1)} %all-to-all-done.refs_0_.refs_1_.k_ref.v_ref, f32[2,256,1]{2,1,0:T(8,128)S(1)} %copy.15.refs_2_, f32[3,2,256,512]{3,2,1,0:T(8,128)} %refs_1_.1), custom_call_target="tpu_custom_call" | custom-call | tf_op jit(solution)/shard_map/gradient/pallas_call | solution.py:170
  74.7 43.8 %all_to_all.20 = f32[16,48,512]{2,1,0:T(8,128)S(1)} all-to-all(f32[16,48,512]{2,1,0:T(8,128)S(1)} %bitcast.38), channel_id=1, replica_groups=mesh['x'=4,'y'=4,'zh'=2,'core'=2,'head'=4] {'x','y'}, dimensions={0} | all-to-all | bytes 3145728 | tf_op jit(solution)/shard_map/all_to_all | solution.py:341
  118.6 5.6 %collective-permute-start.4 = (f32[48,512]{1,0:T(8,128)S(1)}, f32[48,512]{1,0:T(8,128)S(1)}, u32[]{:S(2)}, u32[]{:S(2)}) collective-permute-start(f32[48,512]{1,0:T(8,128)S(1)} %reduce_sum.9), channel_id=1, source_target_pairs={{0,8},{8,0},{1,9},{9,1},{2,10},{10,2},{3,11},{11,3},{4,12},{12,4},... | collective-permute-start | bytes 294920 | tf_op jit(solution)/shard_map/ppermute | solution.py:372
  124.2 2.1 collective-permute-done.4
  126.5 41.0 %all_to_all.21 = f32[16,48,512]{2,1,0:T(8,128)} all-to-all(f32[16,48,512]{2,1,0:T(8,128)S(1)} %broadcast_in_dim.7), channel_id=1, replica_groups=mesh['x'=4,'y'=4,'zh'=2,'core'=2,'head'=4] {'x','y'}, dimensions={0} | all-to-all | bytes 3145728 | tf_op jit(solution)/shard_map/all_to_all | solution.py:341
  167.5 7.7 %newton.1.refs_4_.mine_ref = f32[3,256,512]{2,1,0:T(8,128)S(1)} custom-call(s32[1]{0:T(128)} %bitcast.h.head_ref.place_ref, f32[3,256,512]{2,1,0:T(8,128)} %bitcast.39, f32[3,2,256,512]{3,2,1,0:T(8,128)} %refs_1_.1), custom_call_target="tpu_custom_call" | custom-call | tf_op jit(solution)/shard_map/newton/pallas_call | solution.py:190
  175.2 2.6 collective-permute-start.5
  177.8 7.3 %collective-permute-start.6 = (f32[4,2,64,512]{3,2,1,0:T(8,128)S(1)}, f32[4,2,64,512]{3,2,1,0:T(8,128)}, u32[]{:S(2)}, u32[]{:S(2)}) collective-permute-start(f32[4,2,64,512]{3,2,1,0:T(8,128)S(1)} %all-to-all-done.refs_0_.refs_1_.k_ref.v_ref), channel_id=1, source_target_pairs={{0,4},{4,8},{8,12},{12,16},{16,20},{20,24},{24,28},{28,32},{32,36}... | collective-permute-start | bytes 3145736 | tf_op jit(solution)/shard_map/ppermute | solution.py:377
  186.6 2.4 collective-permute-start.2
  189.2 25.3 %collective-permute-done = f32[64,512]{1,0:T(8,128)S(1)} collective-permute-done((f32[64,512]{1,0:T(8,128)}, f32[64,512]{1,0:T(8,128)S(1)}, u32[]{:S(2)}, u32[]{:S(2)}) %collective-permute-start) | collective-permute-done | bytes 131104 | tf_op jit(solution)/shard_map/ppermute | solution.py:345
  214.5 3.0 %collective-permute-done.1 = f32[64,512]{1,0:T(8,128)S(1)} collective-permute-done((f32[64,512]{1,0:T(8,128)S(1)}, f32[64,512]{1,0:T(8,128)S(1)}, u32[]{:S(2)}, u32[]{:S(2)}) %collective-permute-start.1) | collective-permute-done | bytes 131104 | tf_op jit(solution)/shard_map/ppermute | solution.py:345
  217.5 4.1 %attention.1.refs_5_ = f32[256,512]{1,0:T(8,128)S(1)} custom-call(s32[1]{0:T(128)} %bitcast.17.first_ref, s32[4]{0:T(128)S(1)} %pad_add_fusion.order_ref, f32[4,64,512]{2,1,0:T(8,128)S(1)} %pad_maximum_fusion.2.qa.qb.qc.qd.refs_0_.refs_1_.refs_2_.refs_3_, f32[4,64,512]{2,1,0:T(8,128)S(1)} %pad_maximum_fusion.2.qa.qb.qc.qd.refs_0_.refs_1_.refs_2_.refs_3_, ...), custom_call_target="tpu_custom_call" | custom-call | tf_op jit(solution)/shard_map/attention/pallas_call | solution.py:214
  221.6 1.8 shard_map.86.refs_7_
  223.4 3.2 %shard_map.87 = f32[4,64,512]{2,1,0:T(8,128)S(1)} custom-call(s32[1]{0:T(128)} %bitcast.5.h.head_ref, s32[4]{0:T(128)S(1)} %pad_add_fusion.order_ref, f32[4,64,512]{2,1,0:T(8,128)S(1)} %pad_maximum_fusion.2.qa.qb.qc.qd.refs_0_.refs_1_.refs_2_.refs_3_, f32[4,64,512]{2,1,0:T(8,128)S(1)} %pad_maximum_fusion.2.qa.qb.qc.qd.refs_0_.refs_1_.refs_2_.refs_3_, ...), custom_call_target="tpu_custom_call" | custom-call | tf_op jit(solution)/shard_map/pallas_call | solution.py:244
  226.6 18.4 %all_to_all.22.refs_0_.refs_1_.refs_2_.refs_3_ = f32[4,64,512]{2,1,0:T(8,128)S(1)} all-to-all(f32[4,64,512]{2,1,0:T(8,128)S(1)} %shard_map.87), channel_id=1, replica_groups=mesh['x'=4,'y'=4,'zh'=2,'core'=2,'head'=4] {'head'}, dimensions={0} | all-to-all | bytes 1048576 | tf_op jit(solution)/shard_map/all_to_all | solution.py:341
  247.9 6.7 %project.1 = (f32[64,2048]{1,0:T(8,128)S(1)}, f32[64,2048]{1,0:T(8,128)S(1)}) custom-call(s32[1]{0:T(128)} %bitcast.h.head_ref.place_ref, s32[4]{0:T(128)S(1)} %pad_add_fusion.order_ref, f32[4,64,512]{2,1,0:T(8,128)S(1)} %all_to_all.22.refs_0_.refs_1_.refs_2_.refs_3_, f32[4,64,512]{2,1,0:T(8,128)S(1)} %all_to_all.22.refs_0_.refs_1_.refs_2_.refs_3_, ...), custom_call_target="tpu_custom_call" | custom-call | tf_op jit(solution)/shard_map/project/pallas_call | solution.py:283
  255.1 4.3 %assemble.1 = f32[3,2,256,512]{3,2,1,0:T(8,128)} custom-call(s32[1]{0:T(128)} %bitcast.h.head_ref.place_ref, f32[3,256,512]{2,1,0:T(8,128)} %copy-done, f32[3,256,512]{2,1,0:T(8,128)} %collective-permute-done.5.refs_4_.given_ref), custom_call_target="tpu_custom_call" | custom-call | tf_op jit(solution)/shard_map/assemble/pallas_call | solution.py:321
  (42 shorter events, 12.5 us)
Async XLA Ops:
  7.2 240.8 %all-gather.3.cloned.1.call-start = ((), (), s32[]{:S(2)}) async-start(), calls=%async_computation.4 | async-start | bytes 13369344 | tf_op jit(solution)/shard_map/all_gather | solution.py:389
  8.8 24.3 %copy-start.3 = (f32[64,2048]{1,0:T(8,128)S(1)}, f32[64,2048]{1,0:T(8,128)}, u32[]{:S(2)}) copy-start(f32[64,2048]{1,0:T(8,128)} %param.9) | copy-start | bytes 1572868
  8.8 24.3 %copy-start.4 = (f32[64,2048]{1,0:T(8,128)S(1)}, f32[64,2048]{1,0:T(8,128)}, u32[]{:S(2)}) copy-start(f32[64,2048]{1,0:T(8,128)} %param.8) | copy-start | bytes 1572868
  8.8 10.4 %collective-permute-start.8 = (f32[32,2048]{1,0:T(8,128)S(1)}, f32[32,2048]{1,0:T(8,128)S(1)}, u32[]{:S(2)}, u32[]{:S(2)}) collective-permute-start(f32[32,2048]{1,0:T(8,128)S(1)} %weight_slice.1), channel_id=1, source_target_pairs={{0,1},{1,2},{2,3},{3,0},{4,5},{5,6},{6,7},{7,4},{8,9},{9,10},{10,1... | collective-permute-start | bytes 786440 | tf_op jit(solution)/shard_map/ppermute | solution.py:345
  11.3 20.8 %collective-permute-start.9 = (f32[32,2048]{1,0:T(8,128)S(1)}, f32[32,2048]{1,0:T(8,128)S(1)}, u32[]{:S(2)}, u32[]{:S(2)}) collective-permute-start(f32[32,2048]{1,0:T(8,128)S(1)} %weight_slice.1), channel_id=1, source_target_pairs={{0,2},{1,3},{2,0},{3,1},{4,6},{5,7},{6,4},{7,5},{8,10},{9,11},{10,... | collective-permute-start | bytes 786440 | tf_op jit(solution)/shard_map/ppermute | solution.py:345
  14.3 17.8 %collective-permute-start.10 = (f32[32,2048]{1,0:T(8,128)S(1)}, f32[32,2048]{1,0:T(8,128)S(1)}, u32[]{:S(2)}, u32[]{:S(2)}) collective-permute-start(f32[32,2048]{1,0:T(8,128)S(1)} %weight_slice.1), channel_id=1, source_target_pairs={{0,3},{1,0},{2,1},{3,2},{4,7},{5,4},{6,5},{7,6},{8,11},{9,8},{10,9... | collective-permute-start | bytes 786440 | tf_op jit(solution)/shard_map/ppermute | solution.py:345
  34.2 7.3 %copy-start.5 = (f32[2,256]{1,0:T(2,128)S(1)}, f32[2,256]{1,0:T(2,128)}, u32[]{:S(2)}) copy-start(f32[2,256]{1,0:T(2,128)} %param.10) | copy-start | bytes 6148
  34.2 32.7 %all-to-all-start = ((f32[4,2,64,512]{3,2,1,0:T(8,128)}), f32[4,2,64,512]{3,2,1,0:T(8,128)S(1)}, u32[]{:S(2)}, u32[]{:S(2)}) async-start(f32[4,2,64,512]{3,2,1,0:T(8,128)} %pad_maximum_fusion), calls=%async_computation | async-start | bytes 2097152 | tf_op jit(solution)/shard_map/all_to_all | solution.py:341
  69.9 4.4 %collective-permute-start.3 = (f32[3,256,512]{2,1,0:T(8,128)S(1)}, f32[3,256,512]{2,1,0:T(8,128)S(1)}, u32[]{:S(2)}, u32[]{:S(2)}) collective-permute-start(f32[3,256,512]{2,1,0:T(8,128)S(1)} %gradient.3), channel_id=1, source_target_pairs={{0,4},{4,0},{1,5},{5,1},{2,6},{6,2},{3,7},{7,3},{8,12},{12,8},{9,1... | collective-permute-start | bytes 4718600 | tf_op jit(solution)/shard_map/ppermute | solution.py:365
  118.6 7.7 %collective-permute-start.4 = (f32[48,512]{1,0:T(8,128)S(1)}, f32[48,512]{1,0:T(8,128)S(1)}, u32[]{:S(2)}, u32[]{:S(2)}) collective-permute-start(f32[48,512]{1,0:T(8,128)S(1)} %reduce_sum.9), channel_id=1, source_target_pairs={{0,8},{8,0},{1,9},{9,1},{2,10},{10,2},{3,11},{11,3},{4,12},{12,4},... | collective-permute-start | bytes 294920 | tf_op jit(solution)/shard_map/ppermute | solution.py:372
  167.5 17.6 %copy-start.2 = (f32[64,2048]{1,0:T(8,128)S(1)}, f32[64,2048]{1,0:T(8,128)}, u32[]{:S(2)}) copy-start(f32[64,2048]{1,0:T(8,128)} %param.7) | copy-start | bytes 1572868
  175.2 46.4 %copy-start = (f32[3,256,512]{2,1,0:T(8,128)}, f32[3,256,512]{2,1,0:T(8,128)S(1)}, u32[]{:S(2)}) copy-start(f32[3,256,512]{2,1,0:T(8,128)S(1)} %newton.1.refs_4_.mine_ref) | copy-start | bytes 4718596
  175.2 48.2 %collective-permute-start.5 = (f32[3,256,512]{2,1,0:T(8,128)S(1)}, f32[3,256,512]{2,1,0:T(8,128)}, u32[]{:S(2)}, u32[]{:S(2)}) collective-permute-start(f32[3,256,512]{2,1,0:T(8,128)S(1)} %newton.1.refs_4_.mine_ref), channel_id=1, source_target_pairs={{0,4},{4,0},{1,5},{5,1},{2,6},{6,2},{3,7},{7,3},{8,12},{12,8},{9,1... | collective-permute-start | bytes 4718600 | tf_op jit(solution)/shard_map/ppermute | solution.py:365
  177.8 39.7 %collective-permute-start.6 = (f32[4,2,64,512]{3,2,1,0:T(8,128)S(1)}, f32[4,2,64,512]{3,2,1,0:T(8,128)}, u32[]{:S(2)}, u32[]{:S(2)}) collective-permute-start(f32[4,2,64,512]{3,2,1,0:T(8,128)S(1)} %all-to-all-done.refs_0_.refs_1_.k_ref.v_ref), channel_id=1, source_target_pairs={{0,4},{4,8},{8,12},{12,16},{16,20},{20,24},{24,28},{28,32},{32,36}... | collective-permute-start | bytes 3145736 | tf_op jit(solution)/shard_map/ppermute | solution.py:377
  185.8 28.7 %collective-permute-start = (f32[64,512]{1,0:T(8,128)}, f32[64,512]{1,0:T(8,128)S(1)}, u32[]{:S(2)}, u32[]{:S(2)}) collective-permute-start(f32[64,512]{1,0:T(8,128)} %get-tuple-element.7), channel_id=1, source_target_pairs={{0,1},{1,2},{2,3},{3,0},{4,5},{5,6},{6,7},{7,4},{8,9},{9,10},{10,1... | collective-permute-start | bytes 393224 | tf_op jit(solution)/shard_map/ppermute | solution.py:345
  186.2 31.2 %collective-permute-start.1 = (f32[64,512]{1,0:T(8,128)S(1)}, f32[64,512]{1,0:T(8,128)S(1)}, u32[]{:S(2)}, u32[]{:S(2)}) collective-permute-start(f32[64,512]{1,0:T(8,128)S(1)} %get-tuple-element.9), channel_id=1, source_target_pairs={{0,2},{1,3},{2,0},{3,1},{4,6},{5,7},{6,4},{7,5},{8,10},{9,11},{10,... | collective-permute-start | bytes 393224 | tf_op jit(solution)/shard_map/ppermute | solution.py:345
  186.6 30.8 %collective-permute-start.2 = (f32[64,512]{1,0:T(8,128)S(1)}, f32[64,512]{1,0:T(8,128)S(1)}, u32[]{:S(2)}, u32[]{:S(2)}) collective-permute-start(f32[64,512]{1,0:T(8,128)S(1)} %get-tuple-element.8), channel_id=1, source_target_pairs={{0,3},{1,0},{2,1},{3,2},{4,7},{5,4},{6,5},{7,6},{8,11},{9,8},{10,9... | collective-permute-start | bytes 393224 | tf_op jit(solution)/shard_map/ppermute | solution.py:345
  217.5 4.1 %copy-start.1 = (f32[512]{0:T(512)S(1)}, f32[512]{0:T(512)}, u32[]{:S(2)}) copy-start(f32[512]{0:T(512)} %param.12) | copy-start | bytes 6148
  245.0 2.9 %collective-permute-start.7 = (f32[4,64,512]{2,1,0:T(8,128)S(1)}, f32[4,64,512]{2,1,0:T(8,128)S(1)}, u32[]{:S(2)}, u32[]{:S(2)}) collective-permute-start(f32[4,64,512]{2,1,0:T(8,128)S(1)} %all_to_all.22.refs_0_.refs_1_.refs_2_.refs_3_), channel_id=1, source_target_pairs={{0,4},{4,0},{1,5},{5,1},{2,6},{6,2},{3,7},{7,3},{8,12},{12,8},{9,1... | collective-permute-start | bytes 1572872 | tf_op jit(solution)/shard_map/ppermute | solution.py:365
  254.7 4.8 %collective-permute-start.11 = (f32[64,2048]{1,0:T(8,128)S(1)}, f32[64,2048]{1,0:T(8,128)S(1)}, u32[]{:S(2)}, u32[]{:S(2)}) collective-permute-start(f32[64,2048]{1,0:T(8,128)S(1)} %get-tuple-element.5), channel_id=1, source_target_pairs={{0,4},{4,0},{1,5},{5,1},{2,6},{6,2},{3,7},{7,3},{8,12},{12,8},{9,1... | collective-permute-start | bytes 1572872 | tf_op jit(solution)/shard_map/ppermute | solution.py:365
Sparse Core Ops, SparseCore 0:
  33.2 132.4 all-gather.2
where the time goes:
time: 268 us; the launch traced here: 267 us
  blocking collectives  103 us (38%)
  waiting for transfers between devices  74.3 us (28%)
  Pallas kernels  36.2 us (14%)
  starting transfers between devices  35.5 us (13%)
  between operations  14.3 us (5%)
    all_to_all x3, blocking collectives, exchange(): return lax.all_to_all(value, axes, split_axis=0, concat_axis=0, tiled=True)  103 us
    ppermute x6, waiting for transfers between devices, turned(): lax.ppermute(value, 'head', [(rank, (rank + step) % 4) for rank in range(...  45.3 us
    all_to_all x1, waiting for transfers between devices, exchange(): return lax.all_to_all(value, axes, split_axis=0, concat_axis=0, tiled=True)  25.2 us
    ppermute x6, starting transfers between devices, turned(): lax.ppermute(value, 'head', [(rank, (rank + step) % 4) for rank in range(...  9.52 us
    pallas_call x1, Pallas kernels, newton(): pl.pallas_call(lambda h, *refs: newton_kernel(*refs), grid_spec=spec, out...  7.69 us
    all_to_all x1, starting transfers between devices, exchange(): return lax.all_to_all(value, axes, split_axis=0, concat_axis=0, tiled=True)  7.3 us
    ppermute x1, starting transfers between devices, earlier(): lax.ppermute(value, SEQ, [(source, source + 1) for source in range(63)])  7.27 us
    pallas_call x1, Pallas kernels, project(): pl.pallas_call(project_kernel, grid_spec=pltpu.PrefetchScalarGridSpec(num...  6.73 us
  transfers between devices with their start and end apart: 14, of which 7 were waited for; matrix products, arithmetic and copies ran while one was open for 1% of the time, Pallas kernels for 10%

commit v1 on v0

--- a/solution.py
+++ b/solution.py
@@ -120,11 +120,20 @@
 
 
 def project_kernel(place_ref, order_ref, *refs):
-    lefts, (far_ref, near_ref, mine_ref, theirs_ref) = refs[:8], refs[8:]
+    lefts, (far_ref, edge_ref, near_ref, mine_ref, theirs_ref) = refs[:8], refs[8:]
+    edge = edge_ref.shape[1]
+    piece = (far_ref.shape[1] + edge) // 3
     total = None
     for slot in range(4):
         rows = jnp.concatenate([lefts[slot][...], lefts[4 + slot][...]], axis=0)
-        right = near_ref[...] if slot == 0 else rows_of(far_ref.at[:, slot - 1]).astype(jnp.bfloat16)
+        if slot == 0:
+            right = near_ref[...]
+        elif slot == 3:
+            parts = [far_ref[:, 2 * piece :], edge_ref[...]]
+            right = jnp.concatenate(parts, axis=1).reshape(near_ref.shape).astype(jnp.bfloat16)
+        else:
+            parts = far_ref[:, (slot - 1) * piece : slot * piece]
+            right = parts.reshape(near_ref.shape).astype(jnp.bfloat16)
         value = jnp.dot(rows.astype(jnp.bfloat16), right, preferred_element_type=jnp.float32)
         total = value if total is None else total + value
     half = total.shape[0] // 2
@@ -149,6 +158,7 @@
 
 SEQ = ("x", "y", "zh", "core")
 HEAD_DIM = 256
+EDGE = 8
 PARAMS = pltpu.CompilerParams(vmem_limit_bytes=24 * 2**20)
 
 
@@ -222,7 +232,7 @@
         out_shape=jax.ShapeDtypeStruct((length, width), jnp.float32),
         compiler_params=PARAMS,
         name="attention",
-    )(first, order, *[queries] * 4, before, pairs, before, pairs)
+    )(first, order, *[queries] * 4, in_hbm(before), pairs, in_hbm(before), pairs)
 
 
 def apply_fast(head, order, queries, weights, attended, gain, done=None):
@@ -271,9 +281,27 @@
     )(place, in_hbm(w_out))
 
 
-def project(core, order, mine, theirs, far, near):
+def weight_edge(w_out, core):
+    rows, width = w_out.shape[0] // 16, w_out.shape[1] // 2
+    return pl.pallas_call(
+        slice_kernel,
+        grid_spec=pltpu.PrefetchScalarGridSpec(
+            num_scalar_prefetch=1,
+            grid=(1,),
+            in_specs=[
+                pl.BlockSpec((16, EDGE, width), lambda i, c: (0, rows // EDGE - 1, c[0]))
+            ],
+            out_specs=pl.BlockSpec((16, EDGE, width), lambda i, c: (0, 0, 0)),
+        ),
+        out_shape=jax.ShapeDtypeStruct((16, EDGE, width), jnp.float32),
+        compiler_params=PARAMS,
+        name="weight_edge",
+    )(core, in_hbm(w_out.reshape(16, rows, w_out.shape[1])))
+
+
+def project(core, order, mine, theirs, far, edge, near):
     _, rows, dim = mine.shape
-    parts, others, piece, width = far.shape
+    parts, kept, width = far.shape
     block = width // 4
 
     def left(slot):
@@ -287,7 +315,8 @@
             grid=(width // block,),
             in_specs=[
                 *[left(slot) for slot in range(4)] * 2,
-                pl.BlockSpec((parts, others, piece, block), lambda i, c, order: (0, 0, 0, i)),
+                pl.BlockSpec((parts, kept, block), lambda i, c, order: (0, 0, i)),
+                pl.BlockSpec((parts, edge.shape[1], block), lambda i, c, order: (0, 0, i)),
                 pl.BlockSpec((dim, block), lambda i, c, order: (0, c[0] * (width // block) + i)),
             ],
             out_specs=[out, out],
@@ -295,7 +324,7 @@
         out_shape=[jax.ShapeDtypeStruct((rows, width), jnp.float32)] * 2,
         compiler_params=pltpu.CompilerParams(vmem_limit_bytes=40 * 2**20),
         name="project",
-    )(core, order, *[mine] * 4, *[theirs] * 4, in_hbm(far), in_hbm(near))
+    )(core, order, *[mine] * 4, *[theirs] * 4, in_hbm(far), in_hbm(edge), in_hbm(near))
 
 
 def finish(core, mine, given):
@@ -385,8 +414,11 @@
     gain = norm_gain.reshape(1, -1)
     pairs = exchange(jnp.stack([by_head(k_rows), by_head(v_rows)], axis=1), "head")
     part = weight_slice(w_out, lax.axis_index("x") * 4 + lax.axis_index("y"), core)
-    far_part = jnp.stack([turned(part, step) for step in (1, 2, 3)])
+    steps_part = (part, part, part[:-EDGE])
+    far_part = jnp.concatenate([turned(value, step) for step, value in enumerate(steps_part, 1)])
     far_weights = lax.all_gather(far_part, ("x", "y"))
+    edge_part = weight_edge(w_out, mine)
+    edge = turned(edge_part, 3)
     given = head_gradient(pairs, steps, fast_weights, other)
     received = swap_cores(given)
     kept = head_gradient(pairs, steps, fast_weights, mine)
@@ -401,7 +433,7 @@
     own_rows = exchange(combined, "head")
     their_rows = swap_cores(own_rows)
     turn = jnp.stack([lax.rem(here + 4 - step, 4) for step in range(4)])
-    kept_out, given_out = project(mine, turn, own_rows, their_rows, far_weights, w_out)
+    kept_out, given_out = project(mine, turn, own_rows, their_rows, far_weights, edge, w_out)
     other_half = swap_cores(given_out)
     mixed = finish(mine, kept_out, other_half)
     new_weights = assemble(mine, in_hbm(updated), in_hbm(partner))

time: 268 us -> 282 us (1.052)
  waiting for transfers between devices: 74.3 us -> 99.2 us
  blocking collectives: 103 us -> 80 us
  starting transfers between devices: 35.5 us -> 44.3 us
    all_to_all x3 -> x2, blocking collectives: 103 us -> 80 us  [exchange(): return lax.all_to_all(value, axes, split_axis=0, concat_axis=0, tiled=True)]
    ppermute x6 -> x7, waiting for transfers between devices: 45.3 us -> 62 us  [turned(): lax.ppermute(value, 'head', [(rank, (rank + step) % 4) for rank in range(...]
    all_to_all x1 -> x2, waiting for transfers between devices: 25.2 us -> 35.1 us  [exchange(): return lax.all_to_all(value, axes, split_axis=0, concat_axis=0, tiled=True)]
    all_to_all x1 -> x2, starting transfers between devices: 7.3 us -> 10.9 us  [exchange(): return lax.all_to_all(value, axes, split_axis=0, concat_axis=0, tiled=True)]
    ppermute x6 -> x7, starting transfers between devices: 9.52 us -> 12.9 us  [turned(): lax.ppermute(value, 'head', [(rank, (rank + step) % 4) for rank in range(...]
  transfers between devices with their start and end apart: 14 -> 16, of which waited for: 7 -> 8; matrix products, arithmetic and copies ran while one was open for 1% -> 1% of each run, Pallas kernels for 10% -> 10%
where the time goes in v1:
time: 282 us; the launch traced here: 280 us
  waiting for transfers between devices  99.2 us (35%)
  blocking collectives  80 us (28%)
  starting transfers between devices  44.3 us (16%)
  Pallas kernels  38.1 us (14%)
  between operations  14.3 us (5%)
    all_to_all x2, blocking collectives, exchange(): return lax.all_to_all(value, axes, split_axis=0, concat_axis=0, tiled=True)  80 us
    ppermute x7, waiting for transfers between devices, turned(): lax.ppermute(value, 'head', [(rank, (rank + step) % 4) for rank in range(...  62 us
    all_to_all x2, waiting for transfers between devices, exchange(): return lax.all_to_all(value, axes, split_axis=0, concat_axis=0, tiled=True)  35.1 us
    ppermute x7, starting transfers between devices, turned(): lax.ppermute(value, 'head', [(rank, (rank + step) % 4) for rank in range(...  12.9 us
    all_to_all x2, starting transfers between devices, exchange(): return lax.all_to_all(value, axes, split_axis=0, concat_axis=0, tiled=True)  10.9 us
    pallas_call x1, Pallas kernels, newton(): pl.pallas_call(lambda h, *refs: newton_kernel(*refs), grid_spec=spec, out...  7.7 us
    ppermute x1, starting transfers between devices, earlier(): lax.ppermute(value, SEQ, [(source, source + 1) for source in range(63)])  7.5 us
    ppermute x4, starting transfers between devices, swap_cores(): return lax.ppermute(value, 'core', [(0, 1), (1, 0)])  7.31 us
  transfers between devices with their start and end apart: 16, of which 8 were waited for; matrix products, arithmetic and copies ran while one was open for 1% of the time, Pallas kernels for 10%

profile of v1, /device:TPU:1, one launch (start us, length us, event | category | flops | bytes accessed | tf_op | source)
XLA Modules:
  0.0 279.6 jit_solution(17198715506983343303)
XLA Ops:
  8.8 2.5 collective-permute-start.8
  11.3 3.0 %collective-permute-start.9 = (f32[32,2048]{1,0:T(8,128)S(1)}, f32[32,2048]{1,0:T(8,128)S(1)}, u32[]{:S(2)}, u32[]{:S(2)}) collective-permute-start(f32[32,2048]{1,0:T(8,128)S(1)} %weight_slice.1), channel_id=1, source_target_pairs={{0,2},{1,3},{2,0},{3,1},{4,6},{5,7},{6,4},{7,5},{8,10},{9,11},{10,... | collective-permute-start | bytes 786440 | tf_op jit(solution)/shard_map/ppermute | solution.py:374
  15.1 11.1 %collective-permute-done.10 = f32[24,2048]{1,0:T(8,128)S(1)} collective-permute-done((f32[24,2048]{1,0:T(8,128)S(1)}, f32[24,2048]{1,0:T(8,128)S(1)}, u32[]{:S(2)}, u32[]{:S(2)}) %collective-permute-start.10) | collective-permute-done | bytes 196640 | tf_op jit(solution)/shard_map/ppermute | solution.py:374
  26.2 5.9 %collective-permute-done.9 = f32[32,2048]{1,0:T(8,128)S(1)} collective-permute-done((f32[32,2048]{1,0:T(8,128)S(1)}, f32[32,2048]{1,0:T(8,128)S(1)}, u32[]{:S(2)}, u32[]{:S(2)}) %collective-permute-start.9) | collective-permute-done | bytes 262176 | tf_op jit(solution)/shard_map/ppermute | solution.py:374
  34.2 5.9 %all-to-all-start = ((f32[4,2,64,512]{3,2,1,0:T(8,128)}), f32[4,2,64,512]{3,2,1,0:T(8,128)S(1)}, u32[]{:S(2)}, u32[]{:S(2)}) async-start(f32[4,2,64,512]{3,2,1,0:T(8,128)} %pad_maximum_fusion), calls=%async_computation | async-start | bytes 2097152 | tf_op jit(solution)/shard_map/all_to_all | solution.py:370
  40.2 25.2 %all-to-all-done.refs_0_.refs_1_.k_ref.v_ref = f32[4,2,64,512]{3,2,1,0:T(8,128)S(1)} async-done(((f32[4,2,64,512]{3,2,1,0:T(8,128)}), f32[4,2,64,512]{3,2,1,0:T(8,128)S(1)}, u32[]{:S(2)}, u32[]{:S(2)}) %all-to-all-start) | async-done | bytes 1048608 | tf_op jit(solution)/shard_map/all_to_all | solution.py:370
  65.5 3.0 %gradient.3 = f32[3,256,512]{2,1,0:T(8,128)S(1)} custom-call(s32[1]{0:T(128)} %bitcast.5.h.head_ref, f32[4,2,64,512]{3,2,1,0:T(8,128)S(1)} %all-to-all-done.refs_0_.refs_1_.k_ref.v_ref, f32[4,2,64,512]{3,2,1,0:T(8,128)S(1)} %all-to-all-done.refs_0_.refs_1_.k_ref.v_ref, f32[2,256,1]{2,1,0:T(8,128)S(1)} %copy.11.refs_2_, f32[3,2,256,512]{3,2,1,0:T(8,128)} %refs_1_.1), custom_call_target="tpu_custom_call" | custom-call | tf_op jit(solution)/shard_map/gradient/pallas_call | solution.py:180
  69.9 3.0 %gradient.2 = f32[3,256,512]{2,1,0:T(8,128)S(1)} custom-call(s32[1]{0:T(128)} %bitcast.h.head_ref.place_ref, f32[4,2,64,512]{3,2,1,0:T(8,128)S(1)} %all-to-all-done.refs_0_.refs_1_.k_ref.v_ref, f32[4,2,64,512]{3,2,1,0:T(8,128)S(1)} %all-to-all-done.refs_0_.refs_1_.k_ref.v_ref, f32[2,256,1]{2,1,0:T(8,128)S(1)} %copy.11.refs_2_, f32[3,2,256,512]{3,2,1,0:T(8,128)} %refs_1_.1), custom_call_target="tpu_custom_call" | custom-call | tf_op jit(solution)/shard_map/gradient/pallas_call | solution.py:180
  73.3 43.9 %all_to_all.20 = f32[16,48,512]{2,1,0:T(8,128)S(1)} all-to-all(f32[16,48,512]{2,1,0:T(8,128)S(1)} %bitcast.37), channel_id=1, replica_groups=mesh['x'=4,'y'=4,'zh'=2,'core'=2,'head'=4] {'x','y'}, dimensions={0} | all-to-all | bytes 3145728 | tf_op jit(solution)/shard_map/all_to_all | solution.py:370
  117.2 5.6 %collective-permute-start.4 = (f32[48,512]{1,0:T(8,128)S(1)}, f32[48,512]{1,0:T(8,128)S(1)}, u32[]{:S(2)}, u32[]{:S(2)}) collective-permute-start(f32[48,512]{1,0:T(8,128)S(1)} %reduce_sum.9), channel_id=1, source_target_pairs={{0,8},{8,0},{1,9},{9,1},{2,10},{10,2},{3,11},{11,3},{4,12},{12,4},... | collective-permute-start | bytes 294920 | tf_op jit(solution)/shard_map/ppermute | solution.py:401
  125.1 36.1 %all_to_all.21 = f32[16,48,512]{2,1,0:T(8,128)} all-to-all(f32[16,48,512]{2,1,0:T(8,128)S(1)} %broadcast_in_dim.7), channel_id=1, replica_groups=mesh['x'=4,'y'=4,'zh'=2,'core'=2,'head'=4] {'x','y'}, dimensions={0} | all-to-all | bytes 3145728 | tf_op jit(solution)/shard_map/all_to_all | solution.py:370
  161.2 7.7 %newton.1.refs_4_.mine_ref = f32[3,256,512]{2,1,0:T(8,128)S(1)} custom-call(s32[1]{0:T(128)} %bitcast.h.head_ref.place_ref, f32[3,256,512]{2,1,0:T(8,128)} %bitcast.38, f32[3,2,256,512]{3,2,1,0:T(8,128)} %refs_1_.1), custom_call_target="tpu_custom_call" | custom-call | tf_op jit(solution)/shard_map/newton/pallas_call | solution.py:200
  169.0 2.9 %collective-permute-start.5 = (f32[3,256,512]{2,1,0:T(8,128)S(1)}, f32[3,256,512]{2,1,0:T(8,128)}, u32[]{:S(2)}, u32[]{:S(2)}) collective-permute-start(f32[3,256,512]{2,1,0:T(8,128)S(1)} %newton.1.refs_4_.mine_ref), channel_id=1, source_target_pairs={{0,4},{4,0},{1,5},{5,1},{2,6},{6,2},{3,7},{7,3},{8,12},{12,8},{9,1... | collective-permute-start | bytes 4718600 | tf_op jit(solution)/shard_map/ppermute | solution.py:394
  171.9 7.5 %collective-permute-start.6 = (f32[4,2,64,512]{3,2,1,0:T(8,128)S(1)}, f32[4,2,64,512]{3,2,1,0:T(8,128)}, u32[]{:S(2)}, u32[]{:S(2)}) collective-permute-start(f32[4,2,64,512]{3,2,1,0:T(8,128)S(1)} %all-to-all-done.refs_0_.refs_1_.k_ref.v_ref), channel_id=1, source_target_pairs={{0,4},{4,8},{8,12},{12,16},{16,20},{20,24},{24,28},{28,32},{32,36}... | collective-permute-start | bytes 3145736 | tf_op jit(solution)/shard_map/ppermute | solution.py:406
  183.5 24.9 %collective-permute-done = f32[64,512]{1,0:T(8,128)S(1)} collective-permute-done((f32[64,512]{1,0:T(8,128)}, f32[64,512]{1,0:T(8,128)S(1)}, u32[]{:S(2)}, u32[]{:S(2)}) %collective-permute-start) | collective-permute-done | bytes 131104 | tf_op jit(solution)/shard_map/ppermute | solution.py:374
  208.4 3.0 %collective-permute-done.1 = f32[64,512]{1,0:T(8,128)S(1)} collective-permute-done((f32[64,512]{1,0:T(8,128)S(1)}, f32[64,512]{1,0:T(8,128)S(1)}, u32[]{:S(2)}, u32[]{:S(2)}) %collective-permute-start.1) | collective-permute-done | bytes 131104 | tf_op jit(solution)/shard_map/ppermute | solution.py:374
  211.4 4.1 %attention.1.refs_5_ = f32[256,512]{1,0:T(8,128)S(1)} custom-call(s32[1]{0:T(128)} %bitcast.17.first_ref, s32[4]{0:T(128)S(1)} %pad_add_fusion.order_ref, f32[4,64,512]{2,1,0:T(8,128)S(1)} %pad_maximum_fusion.2.qa.qb.qc.qd.refs_0_.refs_1_.refs_2_.refs_3_, f32[4,64,512]{2,1,0:T(8,128)S(1)} %pad_maximum_fusion.2.qa.qb.qc.qd.refs_0_.refs_1_.refs_2_.refs_3_, ...), custom_call_target="tpu_custom_call" | custom-call | tf_op jit(solution)/shard_map/attention/pallas_call | solution.py:224
  217.3 4.0 %shard_map.87 = f32[4,64,512]{2,1,0:T(8,128)} custom-call(s32[1]{0:T(128)} %bitcast.5.h.head_ref, s32[4]{0:T(128)S(1)} %pad_add_fusion.order_ref, f32[4,64,512]{2,1,0:T(8,128)S(1)} %pad_maximum_fusion.2.qa.qb.qc.qd.refs_0_.refs_1_.refs_2_.refs_3_, f32[4,64,512]{2,1,0:T(8,128)S(1)} %pad_maximum_fusion.2.qa.qb.qc.qd.refs_0_.refs_1_.refs_2_.refs_3_, ...), custom_call_target="tpu_custom_call" | custom-call | tf_op jit(solution)/shard_map/pallas_call | solution.py:254
  221.3 5.0 %all-to-all-start.3 = ((f32[4,64,512]{2,1,0:T(8,128)}), f32[4,64,512]{2,1,0:T(8,128)S(1)}, u32[]{:S(2)}, u32[]{:S(2)}) async-start(f32[4,64,512]{2,1,0:T(8,128)} %shard_map.87), calls=%async_computation.3 | async-start | bytes 1048576 | tf_op jit(solution)/shard_map/all_to_all | solution.py:370
  227.4 3.3 %collective-permute-start.11 = (f32[16,8,2048]{2,1,0:T(8,128)S(1)}, f32[16,8,2048]{2,1,0:T(8,128)}, u32[]{:S(2)}, u32[]{:S(2)}) collective-permute-start(f32[16,8,2048]{2,1,0:T(8,128)S(1)} %weight_edge.1), channel_id=1, source_target_pairs={{0,3},{1,0},{2,1},{3,2},{4,7},{5,4},{6,5},{7,6},{8,11},{9,8},{10,9... | collective-permute-start | bytes 3145736 | tf_op jit(solution)/shard_map/ppermute | solution.py:374
  230.8 9.9 %all-to-all-done.3.refs_0_.refs_1_.refs_2_.refs_3_ = f32[4,64,512]{2,1,0:T(8,128)S(1)} async-done(((f32[4,64,512]{2,1,0:T(8,128)}), f32[4,64,512]{2,1,0:T(8,128)S(1)}, u32[]{:S(2)}, u32[]{:S(2)}) %all-to-all-start.3) | async-done | bytes 524320 | tf_op jit(solution)/shard_map/all_to_all | solution.py:370
  242.5 17.2 %collective-permute-done.11.refs_9_ = f32[16,8,2048]{2,1,0:T(8,128)} collective-permute-done((f32[16,8,2048]{2,1,0:T(8,128)S(1)}, f32[16,8,2048]{2,1,0:T(8,128)}, u32[]{:S(2)}, u32[]{:S(2)}) %collective-permute-start.11) | collective-permute-done | bytes 1048608 | tf_op jit(solution)/shard_map/ppermute | solution.py:374
  259.7 6.8 %project.1 = (f32[64,2048]{1,0:T(8,128)S(1)}, f32[64,2048]{1,0:T(8,128)S(1)}) custom-call(s32[1]{0:T(128)} %bitcast.h.head_ref.place_ref, s32[4]{0:T(128)S(1)} %pad_add_fusion.order_ref, f32[4,64,512]{2,1,0:T(8,128)S(1)} %all-to-all-done.3.refs_0_.refs_1_.refs_2_.refs_3_, f32[4,64,512]{2,1,0:T(8,128)S(1)} %all-to-all-done.3.refs_0_.refs_1_.refs_2_.refs_3_, ...), custom_call_target="tpu_custom_call" | custom-call | tf_op jit(solution)/shard_map/project/pallas_call | solution.py:311
  267.6 4.3 %assemble.1 = f32[3,2,256,512]{3,2,1,0:T(8,128)} custom-call(s32[1]{0:T(128)} %bitcast.h.head_ref.place_ref, f32[3,256,512]{2,1,0:T(8,128)} %copy-done, f32[3,256,512]{2,1,0:T(8,128)} %collective-permute-done.5.refs_4_.given_ref), custom_call_target="tpu_custom_call" | custom-call | tf_op jit(solution)/shard_map/assemble/pallas_call | solution.py:350
  (47 shorter events, 19.7 us)
Async XLA Ops:
  7.2 252.5 %all-gather.3.cloned.1.call-start = ((), (), s32[]{:S(2)}) async-start(), calls=%async_computation.4 | async-start | bytes 12255232 | tf_op jit(solution)/shard_map/all_gather | solution.py:419
  8.8 24.3 %copy-start.3 = (f32[64,2048]{1,0:T(8,128)S(1)}, f32[64,2048]{1,0:T(8,128)}, u32[]{:S(2)}) copy-start(f32[64,2048]{1,0:T(8,128)} %param.9) | copy-start | bytes 1572868
  8.8 24.3 %copy-start.4 = (f32[64,2048]{1,0:T(8,128)S(1)}, f32[64,2048]{1,0:T(8,128)}, u32[]{:S(2)}) copy-start(f32[64,2048]{1,0:T(8,128)} %param.8) | copy-start | bytes 1572868
  8.8 17.4 %collective-permute-start.8 = (f32[32,2048]{1,0:T(8,128)S(1)}, f32[32,2048]{1,0:T(8,128)S(1)}, u32[]{:S(2)}, u32[]{:S(2)}) collective-permute-start(f32[32,2048]{1,0:T(8,128)S(1)} %weight_slice.1), channel_id=1, source_target_pairs={{0,1},{1,2},{2,3},{3,0},{4,5},{5,6},{6,7},{7,4},{8,9},{9,10},{10,1... | collective-permute-start | bytes 786440 | tf_op jit(solution)/shard_map/ppermute | solution.py:374
  11.3 20.8 %collective-permute-start.9 = (f32[32,2048]{1,0:T(8,128)S(1)}, f32[32,2048]{1,0:T(8,128)S(1)}, u32[]{:S(2)}, u32[]{:S(2)}) collective-permute-start(f32[32,2048]{1,0:T(8,128)S(1)} %weight_slice.1), channel_id=1, source_target_pairs={{0,2},{1,3},{2,0},{3,1},{4,6},{5,7},{6,4},{7,5},{8,10},{9,11},{10,... | collective-permute-start | bytes 786440 | tf_op jit(solution)/shard_map/ppermute | solution.py:374
  14.3 11.9 %collective-permute-start.10 = (f32[24,2048]{1,0:T(8,128)S(1)}, f32[24,2048]{1,0:T(8,128)S(1)}, u32[]{:S(2)}, u32[]{:S(2)}) collective-permute-start(f32[24,2048]{1,0:T(8,128)S(1)} %slice.4), channel_id=1, source_target_pairs={{0,3},{1,0},{2,1},{3,2},{4,7},{5,4},{6,5},{7,6},{8,11},{9,8},{10,9... | collective-permute-start | bytes 589832 | tf_op jit(solution)/shard_map/ppermute | solution.py:374
  34.2 5.9 %copy-start.5 = (f32[2,256]{1,0:T(2,128)S(1)}, f32[2,256]{1,0:T(2,128)}, u32[]{:S(2)}) copy-start(f32[2,256]{1,0:T(2,128)} %param.10) | copy-start | bytes 6148
  34.2 31.3 %all-to-all-start = ((f32[4,2,64,512]{3,2,1,0:T(8,128)}), f32[4,2,64,512]{3,2,1,0:T(8,128)S(1)}, u32[]{:S(2)}, u32[]{:S(2)}) async-start(f32[4,2,64,512]{3,2,1,0:T(8,128)} %pad_maximum_fusion), calls=%async_computation | async-start | bytes 2097152 | tf_op jit(solution)/shard_map/all_to_all | solution.py:370
  68.5 4.4 %collective-permute-start.3 = (f32[3,256,512]{2,1,0:T(8,128)S(1)}, f32[3,256,512]{2,1,0:T(8,128)S(1)}, u32[]{:S(2)}, u32[]{:S(2)}) collective-permute-start(f32[3,256,512]{2,1,0:T(8,128)S(1)} %gradient.3), channel_id=1, source_target_pairs={{0,4},{4,0},{1,5},{5,1},{2,6},{6,2},{3,7},{7,3},{8,12},{12,8},{9,1... | collective-permute-start | bytes 4718600 | tf_op jit(solution)/shard_map/ppermute | solution.py:394
  117.2 7.7 %collective-permute-start.4 = (f32[48,512]{1,0:T(8,128)S(1)}, f32[48,512]{1,0:T(8,128)S(1)}, u32[]{:S(2)}, u32[]{:S(2)}) collective-permute-start(f32[48,512]{1,0:T(8,128)S(1)} %reduce_sum.9), channel_id=1, source_target_pairs={{0,8},{8,0},{1,9},{9,1},{2,10},{10,2},{3,11},{11,3},{4,12},{12,4},... | collective-permute-start | bytes 294920 | tf_op jit(solution)/shard_map/ppermute | solution.py:401
  161.2 18.2 %copy-start.2 = (f32[64,2048]{1,0:T(8,128)S(1)}, f32[64,2048]{1,0:T(8,128)}, u32[]{:S(2)}) copy-start(f32[64,2048]{1,0:T(8,128)} %param.7) | copy-start | bytes 1572868
  168.9 46.5 %copy-start = (f32[3,256,512]{2,1,0:T(8,128)}, f32[3,256,512]{2,1,0:T(8,128)S(1)}, u32[]{:S(2)}) copy-start(f32[3,256,512]{2,1,0:T(8,128)S(1)} %newton.1.refs_4_.mine_ref) | copy-start | bytes 4718596
  169.0 48.4 %collective-permute-start.5 = (f32[3,256,512]{2,1,0:T(8,128)S(1)}, f32[3,256,512]{2,1,0:T(8,128)}, u32[]{:S(2)}, u32[]{:S(2)}) collective-permute-start(f32[3,256,512]{2,1,0:T(8,128)S(1)} %newton.1.refs_4_.mine_ref), channel_id=1, source_target_pairs={{0,4},{4,0},{1,5},{5,1},{2,6},{6,2},{3,7},{7,3},{8,12},{12,8},{9,1... | collective-permute-start | bytes 4718600 | tf_op jit(solution)/shard_map/ppermute | solution.py:394
  171.9 39.5 %collective-permute-start.6 = (f32[4,2,64,512]{3,2,1,0:T(8,128)S(1)}, f32[4,2,64,512]{3,2,1,0:T(8,128)}, u32[]{:S(2)}, u32[]{:S(2)}) collective-permute-start(f32[4,2,64,512]{3,2,1,0:T(8,128)S(1)} %all-to-all-done.refs_0_.refs_1_.k_ref.v_ref), channel_id=1, source_target_pairs={{0,4},{4,8},{8,12},{12,16},{16,20},{20,24},{24,28},{28,32},{32,36}... | collective-permute-start | bytes 3145736 | tf_op jit(solution)/shard_map/ppermute | solution.py:406
  180.1 28.3 %collective-permute-start = (f32[64,512]{1,0:T(8,128)}, f32[64,512]{1,0:T(8,128)S(1)}, u32[]{:S(2)}, u32[]{:S(2)}) collective-permute-start(f32[64,512]{1,0:T(8,128)} %get-tuple-element.7), channel_id=1, source_target_pairs={{0,1},{1,2},{2,3},{3,0},{4,5},{5,6},{6,7},{7,4},{8,9},{9,10},{10,1... | collective-permute-start | bytes 393224 | tf_op jit(solution)/shard_map/ppermute | solution.py:374
  180.1 31.2 %collective-permute-start.1 = (f32[64,512]{1,0:T(8,128)S(1)}, f32[64,512]{1,0:T(8,128)S(1)}, u32[]{:S(2)}, u32[]{:S(2)}) collective-permute-start(f32[64,512]{1,0:T(8,128)S(1)} %get-tuple-element.9), channel_id=1, source_target_pairs={{0,2},{1,3},{2,0},{3,1},{4,6},{5,7},{6,4},{7,5},{8,10},{9,11},{10,... | collective-permute-start | bytes 393224 | tf_op jit(solution)/shard_map/ppermute | solution.py:374
  181.0 30.4 %collective-permute-start.2 = (f32[64,512]{1,0:T(8,128)S(1)}, f32[64,512]{1,0:T(8,128)S(1)}, u32[]{:S(2)}, u32[]{:S(2)}) collective-permute-start(f32[64,512]{1,0:T(8,128)S(1)} %get-tuple-element.8), channel_id=1, source_target_pairs={{0,3},{1,0},{2,1},{3,2},{4,7},{5,4},{6,5},{7,6},{8,11},{9,8},{10,9... | collective-permute-start | bytes 393224 | tf_op jit(solution)/shard_map/ppermute | solution.py:374
  211.4 4.1 %copy-start.1 = (f32[512]{0:T(512)S(1)}, f32[512]{0:T(512)}, u32[]{:S(2)}) copy-start(f32[512]{0:T(512)} %param.12) | copy-start | bytes 6148
  221.3 19.3 %all-to-all-start.3 = ((f32[4,64,512]{2,1,0:T(8,128)}), f32[4,64,512]{2,1,0:T(8,128)S(1)}, u32[]{:S(2)}, u32[]{:S(2)}) async-start(f32[4,64,512]{2,1,0:T(8,128)} %shard_map.87), calls=%async_computation.3 | async-start | bytes 1048576 | tf_op jit(solution)/shard_map/all_to_all | solution.py:370
  227.4 32.2 %collective-permute-start.11 = (f32[16,8,2048]{2,1,0:T(8,128)S(1)}, f32[16,8,2048]{2,1,0:T(8,128)}, u32[]{:S(2)}, u32[]{:S(2)}) collective-permute-start(f32[16,8,2048]{2,1,0:T(8,128)S(1)} %weight_edge.1), channel_id=1, source_target_pairs={{0,3},{1,0},{2,1},{3,2},{4,7},{5,4},{6,5},{7,6},{8,11},{9,8},{10,9... | collective-permute-start | bytes 3145736 | tf_op jit(solution)/shard_map/ppermute | solution.py:374
  240.6 19.0 %collective-permute-start.7 = (f32[4,64,512]{2,1,0:T(8,128)S(1)}, f32[4,64,512]{2,1,0:T(8,128)S(1)}, u32[]{:S(2)}, u32[]{:S(2)}) collective-permute-start(f32[4,64,512]{2,1,0:T(8,128)S(1)} %all-to-all-done.3.refs_0_.refs_1_.refs_2_.refs_3_), channel_id=1, source_target_pairs={{0,4},{4,0},{1,5},{5,1},{2,6},{6,2},{3,7},{7,3},{8,12},{12,8},{9,1... | collective-permute-start | bytes 1572872 | tf_op jit(solution)/shard_map/ppermute | solution.py:394
  266.4 5.5 %collective-permute-start.12 = (f32[64,2048]{1,0:T(8,128)S(1)}, f32[64,2048]{1,0:T(8,128)S(1)}, u32[]{:S(2)}, u32[]{:S(2)}) collective-permute-start(f32[64,2048]{1,0:T(8,128)S(1)} %get-tuple-element.5), channel_id=1, source_target_pairs={{0,4},{4,0},{1,5},{5,1},{2,6},{6,2},{3,7},{7,3},{8,12},{12,8},{9,1... | collective-permute-start | bytes 1572872 | tf_op jit(solution)/shard_map/ppermute | solution.py:394
Sparse Core Ops, SparseCore 0:
  33.1 125.4 all-gather.2
